TPU v7x, 32 devices: a whole 2x2x4 slice. The times are simulated.
32 devices in a mesh: grp: 2 (over y), row: 4 (over z), col: 4 (over x, core).
Axes of the slice: x: 2, y: 2, z: 4, core: 2. Of those that a mesh axis runs over, the one named last changes fastest.
Arguments:
- inputs: bfloat16 [256, 16384], P(('grp', 'row'), 'col'), parts along dimension 0, may hold values from -6 to 6
- output_gradient: bfloat16 [256, 16384], P(('grp', 'row'), 'col'), parts along dimension 0, may hold values from -6 to 6
- gate_preactivation: bfloat16 [256, 8192], P('grp', 'row'), parts along dimension 0, may hold values from -6 to 6
- up_preactivation: bfloat16 [256, 8192], P('grp', 'row'), parts along dimension 0, may hold values from -6 to 6
- gate_weight: bfloat16 [16384, 8192], P('col', 'row'), may hold values from -0.046875 to 0.046875
- up_weight: bfloat16 [16384, 8192], P('col', 'row'), may hold values from -0.046875 to 0.046875
- down_weight: bfloat16 [8192, 16384], P('row', 'col'), may hold values from -0.0625 to 0.0625
- up_adapter_entry: bfloat16 [16, 16384], P(None, 'col'), may hold values from -6 to 6
- up_adapter_exit: bfloat16 [16, 8192], P(None, 'row'), may hold values from -0.0032958984 to 0.0032958984
- down_adapter_entry: bfloat16 [16, 8192], P(None, 'row'), may hold values from -6 to 6
- down_adapter_exit: bfloat16 [16, 16384], P(None, 'col'), may hold values from -0.0023956299 to 0.0023956299
- up_adapter_activations: bfloat16 [16, 256], P(None, 'grp'), parts along dimension 1, may hold values from -0.29882812 to 0.29882812
- down_adapter_activations: bfloat16 [16, 256], P(None, 'grp'), parts along dimension 1, may hold values from -0.29882812 to 0.29882812
Outputs:
- grad_inputs: bfloat16 [256, 16384], P(('grp', 'row'), 'col'), parts along dimension 0
- up_entry_gradient: float32 [32, 16384], P('grp', 'col'), parts along dimension 0
- up_exit_gradient: float32 [32, 8192], P('grp', 'row'), parts along dimension 0
- down_entry_gradient: float32 [32, 8192], P('grp', 'row'), parts along dimension 0
- down_exit_gradient: float32 [32, 16384], P('grp', 'col'), parts along dimension 0
There are 2 independent parts, one for each index of `grp`. A program takes and returns all parts, laid end to end along the dimension named above; an argument that names none is the same for every part. Nothing has to cross between parts.
All inputs are finite; a program needn't handle non-finite values.
Results may differ from a plain program's by a relative error of at most 0.005.
Values may be sent and summed in bfloat16 or wider, within the bound.
No kernel may reach another device: no remote copies, remote signals or barrier semaphores. Data moves between devices by JAX's collectives and lax.ppermute only.
A program may use at most 128 MiB of HBM per device.

v0:
```python
import jax
import jax.numpy as jnp
from jax import lax
from jax.sharding import PartitionSpec as P

adapter_scale = 2.0


def contract_trailing(left, right):
    return lax.dot_general(
        left, right, (((1,), (1,)), ((), ())), preferred_element_type=jnp.float32
    )


def contract_leading(left, right, matmul_accuracy=None):
    return lax.dot_general(
        left,
        right,
        (((0,), (0,)), ((), ())),
        precision=matmul_accuracy,
        preferred_element_type=jnp.float32,
    )


def body(
    inputs,
    output_gradient,
    gate_preactivation,
    up_preactivation,
    gate_weight,
    up_weight,
    down_weight,
    up_adapter_entry,
    up_adapter_exit,
    down_adapter_entry,
    down_adapter_exit,
    up_adapter_activations,
    down_adapter_activations,
):
    highest_setting = lax.Precision.HIGHEST
    complete_gradient = lax.all_gather(output_gradient, "row", axis=0, tiled=True)
    down_piece = contract_trailing(complete_gradient, down_adapter_exit)
    hidden_piece = contract_trailing(complete_gradient, down_weight)
    hidden_piece = hidden_piece + adapter_scale * jnp.dot(
        down_piece, down_adapter_entry.astype(jnp.float32), precision=highest_setting
    )
    hidden_gradient, down_full = lax.psum((hidden_piece, down_piece), "col")
    gate_f = gate_preactivation.astype(jnp.float32)
    up_f = up_preactivation.astype(jnp.float32)
    sigmoid_gate = jax.nn.sigmoid(gate_f)
    hidden_state = (gate_f * sigmoid_gate * up_f).astype(jnp.bfloat16)
    gate_grad = (
        hidden_gradient * up_f * sigmoid_gate * (1.0 + gate_f * (1.0 - sigmoid_gate))
    ).astype(jnp.bfloat16)
    up_gradient = (hidden_gradient * gate_f * sigmoid_gate).astype(jnp.bfloat16)
    down_rounded_value = down_full.astype(jnp.bfloat16)
    upper_piece = contract_trailing(up_gradient, up_adapter_exit)
    input_piece = contract_trailing(gate_grad, gate_weight) + contract_trailing(
        up_gradient, up_weight
    )
    input_piece = input_piece + adapter_scale * jnp.dot(
        upper_piece, up_adapter_entry.astype(jnp.float32), precision=highest_setting
    )
    input_grad, upper_full = (
        lax.psum_scatter(input_piece, "row", scatter_dimension=0, tiled=True),
        lax.psum_scatter(upper_piece, "row", scatter_dimension=0, tiled=True),
    )
    up_entry_term = adapter_scale * contract_leading(
        upper_full, inputs.astype(jnp.float32), matmul_accuracy=highest_setting
    )
    up_entry_gradient = lax.psum(up_entry_term, "row")
    up_exit_gradient = adapter_scale * jnp.dot(
        up_adapter_activations, up_gradient, preferred_element_type=jnp.float32
    )
    down_entry_gradient = adapter_scale * contract_leading(down_rounded_value, hidden_state)
    down_exit_gradient = adapter_scale * jnp.dot(
        down_adapter_activations, complete_gradient, preferred_element_type=jnp.float32
    )
    return (
        input_grad.astype(jnp.bfloat16),
        up_entry_gradient,
        up_exit_gradient,
        down_entry_gradient,
        down_exit_gradient,
    )


def solution(mesh):
    placed = (
        P(("grp", "row"), "col"),
        P(("grp", "row"), "col"),
        P("grp", "row"),
        P("grp", "row"),
        P("col", "row"),
        P("col", "row"),
        P("row", "col"),
        P(None, "col"),
        P(None, "row"),
        P(None, "row"),
        P(None, "col"),
        P(None, "grp"),
        P(None, "grp"),
    )
    return jax.shard_map(
        body,
        mesh=mesh,
        in_specs=placed,
        out_specs=(
            P(("grp", "row"), "col"),
            P("grp", "col"),
            P("grp", "row"),
            P("grp", "row"),
            P("grp", "col"),
        ),
        check_vma=False,
    )
```

profile of v0, /device:TPU:0, one launch (start us, length us, event | category | flops | bytes accessed | tf_op | source)
XLA Modules:
  0.0 212.7 jit_solution(2744428697788110122)
XLA Ops:
  7.2 0.0 copy-start
  7.2 0.0 copy-start.5
  7.2 0.0 copy-start.3
  7.2 0.0 copy-start.6
  7.2 0.0 copy-start.7
  7.2 0.0 all-gather.2.cloned.1.call-start
  7.3 0.7 all-gather.2.cloned.1.call-update
  8.0 0.0 all-reduce.3.cloned.1.call-start
  8.0 32.3 %all-gather.2.cloned.1.call-done = bf16[128,4096]{1,0:T(8,128)(2,1)} async-done(((bf16[32,4096]{1,0:T(8,128)(2,1)}), bf16[128,4096]{1,0:T(8,128)(2,1)}) %all-gather.2.cloned.1.call-update) | async-done | bytes 1048592 | tf_op jit(solution)/shard_map/all_gather | solution.py:41
  40.3 1.6 fusion.21
  41.9 11.8 %fusion.20 = f32[128,2048]{1,0:T(8,128)S(1)} fusion(bf16[128,4096]{1,0:T(8,128)(2,1)} %all-gather.2.cloned.1.call-done, bf16[2048,4096]{1,0:T(8,128)(2,1)} %param.19), kind=kOutput, calls=%fused_computation.31 | convolution fusion | flops 2147483648 | bytes 18874368 | tf_op jit(solution)/shard_map/dot_general | solution.py:10
  53.7 0.0 copy-done.5
  53.7 1.6 fusion.1
  55.3 0.0 all-reduce.3.cloned.1.call-update
  55.3 0.0 reduce-scatter.7.cloned.1.call-start
  55.3 35.7 %all-reduce.3.cloned.1.call-done = f32[128,2048]{1,0:T(8,128)} async-done(((f32[128,2048]{1,0:T(8,128)}), f32[128,2048]{1,0:T(8,128)}) %all-reduce.3.cloned.1.call-update) | async-done | bytes 1048592 | tf_op jit(solution)/shard_map/psum | solution.py:47
  91.0 0.0 copy-done.3
  91.0 1.5 fusion.12
  92.5 0.0 copy-start.2
  92.5 0.8 copy-done.2
  93.3 0.0 copy-done.6
  93.3 0.2 fusion.22
  93.6 0.8 copy.18
  94.3 0.0 reduce-scatter.7.cloned.1.call-update
  94.4 0.0 copy-start.4
  94.4 0.2 reduce-scatter.5.cloned.1.call-start
  94.6 0.0 copy-done.7
  94.6 13.2 %fusion.13 = f32[128,4096]{1,0:T(8,128)} fusion(bf16[4096,2048]{1,0:T(8,128)(2,1)} %param.17, f32[128,2048]{1,0:T(8,128)} %all-reduce.3.cloned.1.call-done, bf16[128,2048]{1,0:T(8,128)(2,1)S(1)} %copy-done.7, bf16[128,2048]{1,0:T(8,128)(2,1)S(1)} %copy-done.3), kind=kOutput, calls=%fused_computation.26 | convolution fusion | flops 2150629376 | bytes 20971520 | tf_op jit(solution)/shard_map/dot_general | solution.py:10
  107.8 0.0 copy-start.1
  107.8 12.3 %convolution_add_fusion = f32[128,4096]{1,0:T(8,128)S(1)} fusion(f32[128,4096]{1,0:T(8,128)} %fusion.13, bf16[128,2048]{1,0:T(8,128)(2,1)} %copy-done.2, bf16[4096,2048]{1,0:T(8,128)(2,1)} %param.18), kind=kOutput, calls=%fused_computation.2 | convolution fusion | flops 2148007936 | bytes 21495808 | tf_op jit(solution)/shard_map/dot_general | solution.py:10
  120.1 0.0 copy-done.4
  120.1 2.4 %fusion = f32[128,4096]{1,0:T(8,128)} fusion(f32[128,4096]{1,0:T(8,128)S(1)} %convolution_add_fusion, f32[128,16]{0,1:T(8,128)S(1)} %fusion.22, bf16[16,4096]{1,0:T(8,128)(2,1)S(1)} %copy-done.4), kind=kOutput, calls=%fused_computation.1 | convolution fusion | flops 101711872 | bytes 4333568 | tf_op jit(solution)/shard_map/dot_general | solution.py:61
  122.5 0.0 reduce-scatter.5.cloned.1.call-update
  122.5 0.0 all-reduce.5.cloned.1.call-start
  122.6 6.0 %psum.23 = bf16[128,16]{0,1:T(8,128)(2,1)S(1)} all-reduce(f32[128,16]{0,1:T(8,128)S(1)} %fusion.21), channel_id=1, replica_groups=mesh['grp'=2,'row'=4,'col'=4] {'col'}, use_global_device_ids=true, to_apply=%region_4.0 | all-reduce | flops 2048 | bytes 12288 | tf_op jit(solution)/shard_map/psum | solution.py:47
  128.6 2.4 %convolution_multiply_fusion.5 = f32[16,2048]{1,0:T(8,128)} fusion(bf16[128,2048]{1,0:T(8,128)(2,1)} %param.16, bf16[128,2048]{1,0:T(8,128)(2,1)} %param.15, bf16[128,16]{0,1:T(8,128)(2,1)S(1)} %psum.23), kind=kOutput, calls=%fused_computation.9 | convolution fusion | flops 10518528 | bytes 1183744 | tf_op jit(solution)/shard_map/dot_general | solution.py:16
  131.0 0.0 reduce-scatter.7.cloned.1.call-done
  131.0 0.0 copy-done
  131.0 1.7 convolution_multiply_fusion.2
  132.7 0.0 all-reduce.5.cloned.1.call-update
  132.8 0.0 copy-done.1
  132.8 1.6 convolution_multiply_fusion.1
  134.4 1.9 fusion.2
  136.3 30.6 %reduce-scatter.5.cloned.1.call-done = f32[32,4096]{1,0:T(8,128)} async-done(((f32[128,4096]{1,0:T(8,128)}), f32[32,4096]{1,0:T(8,128)}) %reduce-scatter.5.cloned.1.call-update) | async-done | bytes 524304 | tf_op jit(solution)/shard_map/reduce_scatter | solution.py:65
  166.9 1.8 convert_element_type.28
  168.7 35.8 %all-reduce.5.cloned.1.call-done = f32[16,4096]{1,0:T(8,128)} async-done(((f32[16,4096]{1,0:T(8,128)}), f32[16,4096]{1,0:T(8,128)}) %all-reduce.5.cloned.1.call-update) | async-done | bytes 262160 | tf_op jit(solution)/shard_map/psum | solution.py:71
  204.5 1.7 copy.22
Async XLA Ops:
  7.2 123.8 %copy-start = (bf16[32,4096]{1,0:T(8,128)(2,1)S(1)}, bf16[32,4096]{1,0:T(8,128)(2,1)}, u32[]{:S(2)}) copy-start(bf16[32,4096]{1,0:T(8,128)(2,1)} %param.13) | copy-start | bytes 786436
  7.2 46.5 %copy-start.5 = (bf16[16,2048]{1,0:T(8,128)(2,1)S(1)}, bf16[16,2048]{1,0:T(8,128)(2,1)}, u32[]{:S(2)}) copy-start(bf16[16,2048]{1,0:T(8,128)(2,1)} %param.22) | copy-start | bytes 196612
  7.2 83.8 %copy-start.3 = (bf16[128,2048]{1,0:T(8,128)(2,1)S(1)}, bf16[128,2048]{1,0:T(8,128)(2,1)}, u32[]{:S(2)}) copy-start(bf16[128,2048]{1,0:T(8,128)(2,1)} %param.15) | copy-start | bytes 1572868
  7.2 86.1 %copy-start.6 = (bf16[16,2048]{1,0:T(8,128)(2,1)S(1)}, bf16[16,2048]{1,0:T(8,128)(2,1)}, u32[]{:S(2)}) copy-start(bf16[16,2048]{1,0:T(8,128)(2,1)} %param.21) | copy-start | bytes 196612
  7.2 87.4 %copy-start.7 = (bf16[128,2048]{1,0:T(8,128)(2,1)S(1)}, bf16[128,2048]{1,0:T(8,128)(2,1)}, u32[]{:S(2)}) copy-start(bf16[128,2048]{1,0:T(8,128)(2,1)} %param.16) | copy-start | bytes 1572868
  7.2 33.1 %all-gather.2.cloned.1.call-start = ((), (), s32[]{:S(2)}) async-start(), calls=%async_computation.2 | async-start | bytes 1310720 | tf_op jit(solution)/shard_map/all_gather | solution.py:41
  8.0 83.1 %all-reduce.3.cloned.1.call-start = ((), (), s32[]{:S(2)}) async-start(), calls=%async_computation.3 | async-start | bytes 2097152 | tf_op jit(solution)/shard_map/psum | solution.py:47
  55.3 75.7 %reduce-scatter.7.cloned.1.call-start = ((), (), s32[]{:S(2)}) async-start(), calls=%async_computation.6 | async-start | bytes 81920
  92.5 0.8 copy-start.2
  94.4 25.7 %copy-start.4 = (bf16[16,4096]{1,0:T(8,128)(2,1)S(1)}, bf16[16,4096]{1,0:T(8,128)(2,1)}, u32[]{:S(2)}) copy-start(bf16[16,4096]{1,0:T(8,128)(2,1)} %param.20) | copy-start | bytes 393220
  94.4 72.5 %reduce-scatter.5.cloned.1.call-start = ((), (), s32[]{:S(2)}) async-start(), calls=%async_computation.4 | async-start | bytes 2621440 | tf_op jit(solution)/shard_map/reduce_scatter | solution.py:65
  107.8 25.0 %copy-start.1 = (bf16[128,4096]{1,0:T(8,128)(2,1)S(1)}, bf16[128,4096]{1,0:T(8,128)(2,1)}, u32[]{:S(2)}) copy-start(bf16[128,4096]{1,0:T(8,128)(2,1)} %all-gather.2.cloned.1.call-done) | copy-start | bytes 3145732
  122.5 82.0 %all-reduce.5.cloned.1.call-start = ((), (), s32[]{:S(2)}) async-start(), calls=%async_computation.5 | async-start | bytes 524288 | tf_op jit(solution)/shard_map/psum | solution.py:71
Sparse Core Ops, SparseCore 0:
  9.6 30.6 all-gather.1
  55.4 35.5 all-reduce.2
  94.5 19.4 reduce-scatter.6
  122.6 44.2 reduce-scatter.4
  169.8 34.6 all-reduce.4
where the time goes:
time: 213 us
  waiting for transfers between devices  135 us (63%)
  matrix products  50.8 us (24%)
  between operations  13.9 us (7%)
  blocking collectives  6 us (3%)
  other arithmetic  3.28 us (2%)
  local copies, waits for them, and re-layouts  3.27 us (2%)
    dot_general x5, matrix products, contract_trailing(): lax.dot_general(left, right, (((1,), (1,)), ((), ())), preferred_element_...  39 us
    psum x1, waiting for transfers between devices, body(): up_entry_gradient = lax.psum(up_entry_term, 'row')  35.8 us
    psum x1, waiting for transfers between devices, body(): hidden_gradient, down_full = lax.psum((hidden_piece, down_piece), 'col')  35.7 us
    all_gather x1, waiting for transfers between devices, body(): lax.all_gather(output_gradient, 'row', axis=0, tiled=True)  32.3 us
    reduce_scatter x1, waiting for transfers between devices, body(): lax.psum_scatter(input_piece, 'row', scatter_dimension=0, tiled=True)  30.6 us
    psum x1, blocking collectives, body(): hidden_gradient, down_full = lax.psum((hidden_piece, down_piece), 'col')  6 us
  transfers between devices with their start and end apart: 5, of which 4 were waited for; matrix products, arithmetic and copies ran while one was open for 18% of the time, Pallas kernels for 0%

commit v1 on v0

--- a/solution.py
+++ b/solution.py
@@ -38,7 +38,12 @@
     down_adapter_activations,
 ):
     highest_setting = lax.Precision.HIGHEST
-    complete_gradient = lax.all_gather(output_gradient, "row", axis=0, tiled=True)
+    ring = [output_gradient]
+    for hop in range(3):
+        ring.append(lax.ppermute(ring[-1], "row", [(dev, (dev + 1) % 4) for dev in range(4)]))
+    complete_gradient = jnp.roll(
+        jnp.concatenate(ring[::-1], axis=0), (lax.axis_index("row") + 1) * ring[0].shape[0], axis=0
+    )
     down_piece = contract_trailing(complete_gradient, down_adapter_exit)
     hidden_piece = contract_trailing(complete_gradient, down_weight)
     hidden_piece = hidden_piece + adapter_scale * jnp.dot(

time: 213 us -> 206 us (0.967)
  waiting for transfers between devices: 135 us -> 128 us
  matrix products: 50.8 us -> 46.8 us
  starting transfers between devices: 0.38 us -> 3.43 us
    all_gather x1 -> x0, waiting for transfers between devices: 32.3 us -> none  [body(): lax.all_gather(output_gradient, 'row', axis=0, tiled=True)]
    ppermute x0 -> x3, waiting for transfers between devices: none -> 26.2 us  [body(): lax.ppermute(ring[-1], 'row', [(dev, (dev + 1) % 4) for dev in range(4)])]
    ppermute x0 -> x3, starting transfers between devices: none -> 3.08 us  [body(): lax.ppermute(ring[-1], 'row', [(dev, (dev + 1) % 4) for dev in range(4)])]
  transfers between devices with their start and end apart: 5 -> 7, of which waited for: 4 -> 6; matrix products, arithmetic and copies ran while one was open for 18% -> 17% of each run, Pallas kernels for 0% -> 0%
where the time goes in v1:
time: 206 us
  waiting for transfers between devices  128 us (62%)
  matrix products  46.8 us (23%)
  between operations  14 us (7%)
  blocking collectives  6.01 us (3%)
  local copies, waits for them, and re-layouts  3.59 us (2%)
  other arithmetic  3.5 us (2%)
  starting transfers between devices  3.43 us (2%)
    dot_general x5, matrix products, contract_trailing(): lax.dot_general(left, right, (((1,), (1,)), ((), ())), preferred_element_...  37.9 us
    psum x1, waiting for transfers between devices, body(): up_entry_gradient = lax.psum(up_entry_term, 'row')  35.8 us
    psum x1, waiting for transfers between devices, body(): hidden_gradient, down_full = lax.psum((hidden_piece, down_piece), 'col')  34 us
    reduce_scatter x1, waiting for transfers between devices, body(): lax.psum_scatter(input_piece, 'row', scatter_dimension=0, tiled=True)  32.4 us
    ppermute x3, waiting for transfers between devices, body(): lax.ppermute(ring[-1], 'row', [(dev, (dev + 1) % 4) for dev in range(4)])  26.2 us
    psum x1, blocking collectives, body(): hidden_gradient, down_full = lax.psum((hidden_piece, down_piece), 'col')  6.01 us
  transfers between devices with their start and end apart: 7, of which 6 were waited for; matrix products, arithmetic and copies ran while one was open for 17% of the time, Pallas kernels for 0%

profile of v1, /device:TPU:0, one launch (start us, length us, event | category | flops | bytes accessed | tf_op | source)
XLA Modules:
  0.0 205.7 jit_solution(17854494778632028488)
XLA Ops:
  7.2 0.0 copy-start
  7.2 0.0 copy-start.4
  7.2 0.0 all-reduce.3.cloned.1.call-start
  7.2 3.1 %collective-permute-start = (bf16[32,4096]{1,0:T(8,128)(2,1)}, bf16[32,4096]{1,0:T(8,128)(2,1)S(1)}, u32[]{:S(2)}, u32[]{:S(2)}) collective-permute-start(bf16[32,4096]{1,0:T(8,128)(2,1)} %param.14), channel_id=1, source_target_pairs={{0,4},{4,8},{8,12},{12,0},{1,5},{5,9},{9,13},{13,1},{2,6},{6,10},{... | collective-permute-start | bytes 786440 | tf_op jit(solution)/shard_map/ppermute | solution.py:43
  10.3 8.5 %collective-permute-done = bf16[32,4096]{1,0:T(8,128)(2,1)S(1)} collective-permute-done((bf16[32,4096]{1,0:T(8,128)(2,1)}, bf16[32,4096]{1,0:T(8,128)(2,1)S(1)}, u32[]{:S(2)}, u32[]{:S(2)}) %collective-permute-start) | collective-permute-done | bytes 262176 | tf_op jit(solution)/shard_map/ppermute | solution.py:43
  18.9 0.0 collective-permute-start.1
  18.9 9.3 %collective-permute-done.1 = bf16[32,4096]{1,0:T(8,128)(2,1)S(1)} collective-permute-done((bf16[32,4096]{1,0:T(8,128)(2,1)S(1)}, bf16[32,4096]{1,0:T(8,128)(2,1)S(1)}, u32[]{:S(2)}, u32[]{:S(2)}) %collective-permute-start.1) | collective-permute-done | bytes 262176 | tf_op jit(solution)/shard_map/ppermute | solution.py:43
  28.1 0.0 collective-permute-start.2
  28.2 0.0 copy-start.6
  28.2 8.4 %collective-permute-done.2 = bf16[32,4096]{1,0:T(8,128)(2,1)S(1)} collective-permute-done((bf16[32,4096]{1,0:T(8,128)(2,1)S(1)}, bf16[32,4096]{1,0:T(8,128)(2,1)S(1)}, u32[]{:S(2)}, u32[]{:S(2)}) %collective-permute-start.2) | collective-permute-done | bytes 262176 | tf_op jit(solution)/shard_map/ppermute | solution.py:43
  36.6 0.0 copy-start.8
  36.6 1.0 constant_dynamic-update-slice_fusion.4
  37.7 0.0 copy-done.4
  37.7 0.0 copy-done.6
  37.7 0.0 copy-start.1
  37.7 0.4 fusion.14
  38.1 0.0 copy-done.8
  38.1 0.6 convolution_multiply_fusion.3
  38.7 12.4 %convolution_add_fusion.1 = f32[128,2048]{1,0:T(8,128)} fusion(f32[128,2048]{1,0:T(8,128)S(1)} %convolution_multiply_fusion.3, bf16[2048,4096]{1,0:T(8,128)(2,1)} %param.19, bf16[256,4096]{1,0:T(8,128)(2,1)S(1)} %constant_dynamic-update-slice_fusion, s32[]{:T(128)S(6)} %select_n.14), kind=kOutput, calls=%fused_computation.7 | convolution fusion | flops 2147745792 | bytes 19922948 | tf_op jit(solution)/shard_map/dot_general | solution.py:10
  51.2 0.0 copy-done.1
  51.2 0.0 copy-start.9
  51.2 0.0 copy-start.5
  51.2 0.0 copy-start.12
  51.2 0.0 all-reduce.3.cloned.1.call-update
  51.2 0.0 reduce-scatter.7.cloned.1.call-start
  51.3 34.0 %all-reduce.3.cloned.1.call-done = f32[128,2048]{1,0:T(8,128)} async-done(((f32[128,2048]{1,0:T(8,128)}), f32[128,2048]{1,0:T(8,128)}) %all-reduce.3.cloned.1.call-update) | async-done | bytes 1048592 | tf_op jit(solution)/shard_map/psum | solution.py:52
  85.3 0.0 copy-start.3
  85.3 1.7 fusion.12
  87.0 0.0 copy-done.9
  87.0 0.2 fusion.27
  87.2 0.8 copy.18
  88.0 0.0 reduce-scatter.7.cloned.1.call-update
  88.0 0.2 reduce-scatter.5.cloned.1.call-start
  88.3 0.0 copy-done.5
  88.3 0.0 copy-done.12
  88.3 0.0 copy-done.3
  88.3 12.7 %fusion.17 = f32[128,4096]{1,0:T(8,128)} fusion(bf16[4096,2048]{1,0:T(8,128)(2,1)} %param.17, f32[128,2048]{1,0:T(8,128)S(1)} %copy-done.3, bf16[128,2048]{1,0:T(8,128)(2,1)S(1)} %copy-done.12, bf16[128,2048]{1,0:T(8,128)(2,1)S(1)} %copy-done.5), kind=kOutput, calls=%fused_computation.31 | convolution fusion | flops 2150629376 | bytes 20971520 | tf_op jit(solution)/shard_map/dot_general | solution.py:10
  101.0 0.0 copy-start.7
  101.0 12.1 %convolution_add_fusion = f32[128,4096]{1,0:T(8,128)S(1)} fusion(f32[128,4096]{1,0:T(8,128)} %fusion.17, bf16[128,2048]{1,0:T(8,128)(2,1)S(1)} %fusion.12, bf16[4096,2048]{1,0:T(8,128)(2,1)} %param.18), kind=kOutput, calls=%fused_computation.2 | convolution fusion | flops 2148007936 | bytes 21495808 | tf_op jit(solution)/shard_map/dot_general | solution.py:10
  113.1 0.0 copy-done.7
  113.1 2.4 %fusion = f32[128,4096]{1,0:T(8,128)} fusion(f32[128,4096]{1,0:T(8,128)S(1)} %convolution_add_fusion, f32[128,16]{0,1:T(8,128)S(1)} %fusion.27, bf16[16,4096]{1,0:T(8,128)(2,1)S(1)} %copy-done.7), kind=kOutput, calls=%fused_computation.1 | convolution fusion | flops 101711872 | bytes 4333568 | tf_op jit(solution)/shard_map/dot_general | solution.py:66
  115.5 0.0 reduce-scatter.5.cloned.1.call-update
  115.5 0.0 all-reduce.5.cloned.1.call-start
  115.5 6.0 %psum.23 = bf16[128,16]{0,1:T(8,128)(2,1)S(1)} all-reduce(f32[128,16]{0,1:T(8,128)S(1)} %fusion.14), channel_id=1, replica_groups=mesh['grp'=2,'row'=4,'col'=4] {'col'}, use_global_device_ids=true, to_apply=%region_4.5 | all-reduce | flops 2048 | bytes 12288 | tf_op jit(solution)/shard_map/psum | solution.py:52
  121.6 0.0 copy-start.2
  121.6 0.0 copy-start.10
  121.6 2.3 %convolution_multiply_fusion.5 = f32[16,2048]{1,0:T(8,128)} fusion(bf16[128,2048]{1,0:T(8,128)(2,1)} %param.16, bf16[128,2048]{1,0:T(8,128)(2,1)S(1)} %copy-done.5, bf16[128,16]{0,1:T(8,128)(2,1)S(1)} %psum.23), kind=kOutput, calls=%fused_computation.10 | convolution fusion | flops 10518528 | bytes 1183744 | tf_op jit(solution)/shard_map/dot_general | solution.py:16
  123.9 0.0 copy-start.11
  123.9 0.0 reduce-scatter.7.cloned.1.call-done
  123.9 0.0 copy-done
  123.9 1.7 convolution_multiply_fusion.2
  125.7 0.0 all-reduce.5.cloned.1.call-update
  125.7 0.0 copy-done.2
  125.7 0.0 copy-done.10
  125.7 1.0 fusion.1
  126.7 0.0 copy-done.11
  126.7 0.8 fusion.2
  127.5 32.4 %reduce-scatter.5.cloned.1.call-done = f32[32,4096]{1,0:T(8,128)} async-done(((f32[128,4096]{1,0:T(8,128)}), f32[32,4096]{1,0:T(8,128)}) %reduce-scatter.5.cloned.1.call-update) | async-done | bytes 524304 | tf_op jit(solution)/shard_map/reduce_scatter | solution.py:70
  159.9 1.8 convert_element_type.28
  161.7 35.8 %all-reduce.5.cloned.1.call-done = f32[16,4096]{1,0:T(8,128)} async-done(((f32[16,4096]{1,0:T(8,128)}), f32[16,4096]{1,0:T(8,128)}) %all-reduce.5.cloned.1.call-update) | async-done | bytes 262160 | tf_op jit(solution)/shard_map/psum | solution.py:76
  197.5 1.7 copy.29
  (7 shorter events, 0.1 us)
Async XLA Ops:
  7.2 116.8 %copy-start = (bf16[32,4096]{1,0:T(8,128)(2,1)S(1)}, bf16[32,4096]{1,0:T(8,128)(2,1)}, u32[]{:S(2)}) copy-start(bf16[32,4096]{1,0:T(8,128)(2,1)} %param.13) | copy-start | bytes 786436
  7.2 30.5 %copy-start.4 = (bf16[32,4096]{1,0:T(8,128)(2,1)S(1)}, bf16[32,4096]{1,0:T(8,128)(2,1)}, u32[]{:S(2)}) copy-start(bf16[32,4096]{1,0:T(8,128)(2,1)} %param.14) | copy-start | bytes 786436
  7.2 78.1 %all-reduce.3.cloned.1.call-start = ((), (), s32[]{:S(2)}) async-start(), calls=%async_computation.2 | async-start | bytes 2097152 | tf_op jit(solution)/shard_map/psum | solution.py:52
  7.2 11.6 %collective-permute-start = (bf16[32,4096]{1,0:T(8,128)(2,1)}, bf16[32,4096]{1,0:T(8,128)(2,1)S(1)}, u32[]{:S(2)}, u32[]{:S(2)}) collective-permute-start(bf16[32,4096]{1,0:T(8,128)(2,1)} %param.14), channel_id=1, source_target_pairs={{0,4},{4,8},{8,12},{12,0},{1,5},{5,9},{9,13},{13,1},{2,6},{6,10},{... | collective-permute-start | bytes 786440 | tf_op jit(solution)/shard_map/ppermute | solution.py:43
  18.9 9.3 %collective-permute-start.1 = (bf16[32,4096]{1,0:T(8,128)(2,1)S(1)}, bf16[32,4096]{1,0:T(8,128)(2,1)S(1)}, u32[]{:S(2)}, u32[]{:S(2)}) collective-permute-start(bf16[32,4096]{1,0:T(8,128)(2,1)S(1)} %collective-permute-done), channel_id=1, source_target_pairs={{0,4},{4,8},{8,12},{12,0},{1,5},{5,9},{9,13},{13,1},{2,6},{6,10},{... | collective-permute-start | bytes 786440 | tf_op jit(solution)/shard_map/ppermute | solution.py:43
  28.1 8.4 %collective-permute-start.2 = (bf16[32,4096]{1,0:T(8,128)(2,1)S(1)}, bf16[32,4096]{1,0:T(8,128)(2,1)S(1)}, u32[]{:S(2)}, u32[]{:S(2)}) collective-permute-start(bf16[32,4096]{1,0:T(8,128)(2,1)S(1)} %collective-permute-done.1), channel_id=1, source_target_pairs={{0,4},{4,8},{8,12},{12,0},{1,5},{5,9},{9,13},{13,1},{2,6},{6,10},{... | collective-permute-start | bytes 786440 | tf_op jit(solution)/shard_map/ppermute | solution.py:43
  28.2 9.5 %copy-start.6 = (bf16[16,4096]{1,0:T(8,128)(2,1)S(1)}, bf16[16,4096]{1,0:T(8,128)(2,1)}, u32[]{:S(2)}) copy-start(bf16[16,4096]{1,0:T(8,128)(2,1)} %param.23) | copy-start | bytes 393220
  36.6 1.5 copy-start.8
  37.7 13.5 %copy-start.1 = (bf16[256,4096]{1,0:T(8,128)(2,1)}, bf16[256,4096]{1,0:T(8,128)(2,1)S(1)}, u32[]{:S(2)}) copy-start(bf16[256,4096]{1,0:T(8,128)(2,1)S(1)} %constant_dynamic-update-slice_fusion) | copy-start | bytes 6291460
  51.2 35.8 %copy-start.9 = (bf16[16,2048]{1,0:T(8,128)(2,1)S(1)}, bf16[16,2048]{1,0:T(8,128)(2,1)}, u32[]{:S(2)}) copy-start(bf16[16,2048]{1,0:T(8,128)(2,1)} %param.21) | copy-start | bytes 196612
  51.2 37.1 %copy-start.5 = (bf16[128,2048]{1,0:T(8,128)(2,1)S(1)}, bf16[128,2048]{1,0:T(8,128)(2,1)}, u32[]{:S(2)}) copy-start(bf16[128,2048]{1,0:T(8,128)(2,1)} %param.15) | copy-start | bytes 1572868
  51.2 37.1 %copy-start.12 = (bf16[128,2048]{1,0:T(8,128)(2,1)S(1)}, bf16[128,2048]{1,0:T(8,128)(2,1)}, u32[]{:S(2)}) copy-start(bf16[128,2048]{1,0:T(8,128)(2,1)} %param.16) | copy-start | bytes 1572868
  51.2 72.7 %reduce-scatter.7.cloned.1.call-start = ((), (), s32[]{:S(2)}) async-start(), calls=%async_computation.5 | async-start | bytes 81920
  85.3 3.0 %copy-start.3 = (f32[128,2048]{1,0:T(8,128)S(1)}, f32[128,2048]{1,0:T(8,128)}, u32[]{:S(2)}) copy-start(f32[128,2048]{1,0:T(8,128)} %all-reduce.3.cloned.1.call-done) | copy-start | bytes 3145732
  88.0 71.9 %reduce-scatter.5.cloned.1.call-start = ((), (), s32[]{:S(2)}) async-start(), calls=%async_computation.3 | async-start | bytes 2621440 | tf_op jit(solution)/shard_map/reduce_scatter | solution.py:70
  101.0 12.1 %copy-start.7 = (bf16[16,4096]{1,0:T(8,128)(2,1)S(1)}, bf16[16,4096]{1,0:T(8,128)(2,1)}, u32[]{:S(2)}) copy-start(bf16[16,4096]{1,0:T(8,128)(2,1)} %param.20) | copy-start | bytes 393220
  115.5 82.0 %all-reduce.5.cloned.1.call-start = ((), (), s32[]{:S(2)}) async-start(), calls=%async_computation.4 | async-start | bytes 524288 | tf_op jit(solution)/shard_map/psum | solution.py:76
  121.6 4.1 %copy-start.2 = (bf16[256,4096]{1,0:T(8,128)(2,1)S(1)}, bf16[256,4096]{1,0:T(8,128)(2,1)}, u32[]{:S(2)}) copy-start(bf16[256,4096]{1,0:T(8,128)(2,1)} %copy-done.1) | copy-start | bytes 6291460
  121.6 4.1 %copy-start.10 = (bf16[16,128]{1,0:T(8,128)(2,1)S(1)}, bf16[16,128]{1,0:T(8,128)(2,1)}, u32[]{:S(2)}) copy-start(bf16[16,128]{1,0:T(8,128)(2,1)} %param.25) | copy-start | bytes 12292
  123.9 2.8 %copy-start.11 = (bf16[16,128]{1,0:T(8,128)(2,1)S(1)}, bf16[16,128]{1,0:T(8,128)(2,1)}, u32[]{:S(2)}) copy-start(bf16[16,128]{1,0:T(8,128)(2,1)} %param.24) | copy-start | bytes 12292
Sparse Core Ops, SparseCore 0:
  51.4 33.8 all-reduce.2
  88.2 19.4 reduce-scatter.6
  115.6 44.2 reduce-scatter.4
  162.8 34.6 all-reduce.4
